TPU v7x, 32 devices: a whole 2x2x4 slice. The times are simulated.
32 devices in a mesh: grp: 2 (over y), node: 16 (over z, x, core).
Axes of the slice: x: 2, y: 2, z: 4, core: 2. Of those that a mesh axis runs over, the one named last changes fastest.
Arguments:
- tokens: bfloat16 [128, 7168], P(('grp', 'node')), parts along dimension 0, may hold values from -6 to 6
- routes: int32 [128, 2], P(('grp', 'node')), parts along dimension 0, may hold values from 0 to 3, all different within a row; in each aligned block of 4 rows (0 to 3, 4 to 7, ...) at most 4 rows name the same one
- gates: float32 [128, 2], P(('grp', 'node')), parts along dimension 0, may hold values from 0.05 to 1
- norm_gain: bfloat16 [7168], replicated, may hold values from 0.5 to 1.5
- w_gate: bfloat16 [16, 7168, 256], P('node'), may hold values from -0.0625 to 0.0625
- w_up: bfloat16 [16, 7168, 256], P('node'), may hold values from -0.0625 to 0.0625
- w_down: bfloat16 [16, 256, 7168], P('node'), may hold values from -0.1875 to 0.1875
- queries: bfloat16 [32, 128, 576], P(('grp', 'node')), parts along dimension 0, may hold values from -60 to 60
- cache: bfloat16 [32, 1280, 576], P(('grp', 'node')), parts along dimension 0, may hold values from -6 to 6
- lengths: int32 [32], P(('grp', 'node')), parts along dimension 0, may hold values from 1 to 1280, as said below
Outputs:
- moe_out: bfloat16 [128, 7168], P(('grp', 'node')), parts along dimension 0
- attention_out: bfloat16 [32, 65536], P(('grp', 'node')), parts along dimension 0
There are 2 independent parts, one for each index of `grp`. A program takes and returns all parts, laid end to end along the dimension named above; an argument that names none is the same for every part. Nothing has to cross between parts.
Inputs may be any that keep to these rules, and one draw needn't show every extreme that they name: `routes`: each token names 2 different replicas; within the rows of one device no replica is named by more than 4 tokens. `lengths`: some request has all 1280 positions filled.
All inputs are finite; a program needn't handle non-finite values.
Results may differ from a plain program's by a relative error of at most 0.0077.
Values may be sent and summed in bfloat16 or wider, within the bound.
A program may use at most 128 MiB of HBM per device.

v0:
```python
import jax
import jax.numpy as jnp
from jax import lax
from jax.sharding import PartitionSpec as P

SPLIT = 4
VALUE_DIM = 512


norm_eps = 1e-06
route_scale = 2.5
softmax_scale = 192.0 ** (-0.5)


def per_device(tokens, routes, gates, norm_gain, w_gate, w_up, w_down, queries, cache, lengths):
    row_count = tokens.shape[0]
    pick_count = routes.shape[1]
    width = tokens.shape[1]
    node_count = lax.axis_size("node")
    slot_count = node_count // SPLIT
    capacity = max(2, 2 * row_count * pick_count // slot_count)
    hidden_in = tokens.astype(jnp.float32)
    inverse = lax.rsqrt(jnp.mean(hidden_in * hidden_in, axis=-1, keepdims=True) + norm_eps)
    normed = (hidden_in * inverse * norm_gain.astype(jnp.float32)).astype(jnp.bfloat16)
    mixing = route_scale * gates / jnp.sum(gates, axis=-1, keepdims=True)
    picks_flat = routes.reshape(-1)
    total_picks = row_count * pick_count
    pick_rows = jnp.arange(total_picks, dtype=jnp.int32) // pick_count
    one_hot = (picks_flat[:, None] == jnp.arange(slot_count, dtype=jnp.int32)[None, :]).astype(
        jnp.int32
    )
    rank_in = jnp.sum((jnp.cumsum(one_hot, axis=0) - 1) * one_hot, axis=1)
    placed = picks_flat * capacity + rank_in
    matches = placed[None, :] == jnp.arange(slot_count * capacity, dtype=jnp.int32)[:, None]
    filled = jnp.any(matches, axis=1)
    source_row = jnp.sum(jnp.where(matches, pick_rows[None, :], 0), axis=1)
    slot_rows = jnp.where(filled[:, None], normed[source_row], jnp.zeros((), jnp.bfloat16))
    slot_rows = slot_rows.reshape(slot_count, capacity, width).reshape(
        slot_count, 1, capacity, width
    )
    outgoing = jnp.broadcast_to(slot_rows, (slot_count, SPLIT, capacity, width)).reshape(
        node_count, capacity, width
    )
    arrived = lax.all_to_all(outgoing, "node", split_axis=0, concat_axis=0, tiled=True)
    arrived_shape = arrived.shape
    flat_rows = arrived.reshape(-1, width)
    gate_part = jnp.dot(flat_rows, w_gate[0], preferred_element_type=jnp.float32)
    up_part = jnp.dot(flat_rows, w_up[0], preferred_element_type=jnp.float32)
    hidden = (jax.nn.silu(gate_part) * up_part).astype(jnp.bfloat16)
    result = jnp.dot(hidden, w_down[0], preferred_element_type=jnp.float32).astype(jnp.bfloat16)
    send_result = result.reshape(arrived_shape)
    returned = lax.all_to_all(send_result, "node", split_axis=0, concat_axis=0, tiled=True)
    grouped = returned.reshape(slot_count, SPLIT, capacity, width)
    pieces = grouped[picks_flat, :, rank_in]
    summed = jnp.sum(pieces.astype(jnp.float32), axis=1)
    expert_sum = lax.optimization_barrier(summed.astype(jnp.bfloat16)).astype(jnp.float32)
    expert_sum = expert_sum.reshape(row_count, pick_count, width)
    moe_out = jnp.sum(expert_sum * mixing[:, :, None], axis=1).astype(jnp.bfloat16)
    cache_len = cache.shape[1]
    scores = (
        jnp.einsum("rhc,rjc->rhj", queries, cache, preferred_element_type=jnp.float32)
        * softmax_scale
    )
    valid = jnp.arange(cache_len, dtype=jnp.int32)[None, None, :] < lengths[:, None, None]
    scores = jnp.where(valid, scores, -jnp.inf)
    probs = jax.nn.softmax(scores, axis=-1).astype(jnp.bfloat16)
    attended = jnp.einsum(
        "rhj,rjv->rhv", probs, cache[:, :, :VALUE_DIM], preferred_element_type=jnp.float32
    )
    attention_out = attended.astype(jnp.bfloat16).reshape(queries.shape[0], -1)
    return (moe_out, attention_out)


def solution(mesh):
    in_specs = (
        P(("grp", "node"), None),
        P(("grp", "node"), None),
        P(("grp", "node"), None),
        P(),
        P("node", None, None),
        P("node", None, None),
        P("node", None, None),
        P(("grp", "node"), None, None),
        P(("grp", "node"), None, None),
        P(("grp", "node")),
    )
    out_specs = (P(("grp", "node"), None), P(("grp", "node"), None))
    return jax.shard_map(
        per_device, mesh=mesh, in_specs=in_specs, out_specs=out_specs, check_vma=False
    )
```

profile of v0, /device:TPU:0, one launch (start us, length us, event | category | flops | bytes accessed | tf_op | source)
XLA Modules:
  0.0 73.8 jit_solution(11095684832583081438)
XLA Ops:
  0.6 0.8 %copy.25 = s32[4,2]{1,0:T(4,128)S(1)} copy(s32[4,2]{0,1:T(2,128)} %param.11) | data formatting | bytes 64 | tf_op args[1]
  1.5 0.2 reduce_window_sum.11
  1.9 0.7 convert_element_type.34
  2.7 1.0 %fusion.28 = f32[4]{0:T(128)S(1)} fusion(bf16[4,7168]{1,0:T(4,128)(2,1)} %param.10), kind=kLoop, calls=%fused_computation.28 | loop fusion | flops 86012 | bytes 57360 | tf_op jit(solution)/shard_map/reduce_sum | solution.py:23
  3.7 0.9 %fusion.30 = bf16[4,7168]{1,0:T(4,128)(2,1)S(1)} fusion(bf16[4,7168]{1,0:T(4,128)(2,1)} %param.10, f32[7168]{0:T(1024)S(1)} %convert_element_type.34, f32[4]{0:T(128)S(1)} %add_rsqrt_fusion), kind=kLoop, calls=%fused_computation.30 | loop fusion | flops 114688 | bytes 143376 | tf_op jit(solution)/shard_map/convert_element_type | solution.py:24
  4.6 0.7 gather_fusion
  5.5 0.2 broadcast_select_fusion
  5.6 0.2 broadcast_in_dim.64
  5.9 29.7 %all_to_all.10 = bf16[16,4,7168]{2,1,0:T(4,128)(2,1)S(1)} all-to-all(bf16[16,4,7168]{2,1,0:T(4,128)(2,1)S(1)} %bitcast.53), channel_id=1, replica_groups=mesh['grp'=2,'node'=16] {'node'}, dimensions={0} | all-to-all | bytes 1835008 | tf_op jit(solution)/shard_map/all_to_all | solution.py:44
  35.6 0.2 reshape.173
  35.8 2.8 %fusion.3 = f32[64,256]{1,0:T(8,128)S(1)} fusion(bf16[64,7168]{1,0:T(8,128)(2,1)S(1)} %reshape.173, bf16[1,7168,256]{2,1,0:T(8,128)(2,1)} %param.14), kind=kOutput, calls=%fused_computation.6 | convolution fusion | flops 234881024 | bytes 4653056 | tf_op jit(solution)/shard_map/dot_general | solution.py:47
  38.6 5.5 %convolution_convert_fusion = bf16[64,7168]{1,0:T(8,128)(2,1)S(1)} fusion(bf16[1,256,7168]{2,1,0:T(8,128)(2,1)} %param.16, bf16[64,7168]{1,0:T(8,128)(2,1)S(1)} %reshape.173, bf16[1,7168,256]{2,1,0:T(8,128)(2,1)} %param.15, f32[64,256]{1,0:T(8,128)S(1)} %fusion.3), kind=kOutput, calls=%fused_computation.2 | convolution fusion | flops 470319104 | bytes 9240576 | tf_op jit(solution)/shard_map/dot_general | solution.py:50
  44.1 1.3 %reshape.174 = bf16[16,4,7168]{2,1,0:T(4,128)(2,1)} reshape(bf16[64,7168]{1,0:T(8,128)(2,1)S(1)} %convolution_convert_fusion) | data formatting | bytes 1835008 | tf_op jit(solution)/shard_map/reshape | solution.py:51
  45.3 4.5 %all-to-all-start.1 = ((bf16[16,4,7168]{2,1,0:T(4,128)(2,1)}), bf16[16,4,7168]{2,1,0:T(4,128)(2,1)S(1)}, u32[]{:S(2)}, u32[]{:S(2)}) async-start(bf16[16,4,7168]{2,1,0:T(4,128)(2,1)} %reshape.174), calls=%async_computation.1 | async-start | bytes 1835008 | tf_op jit(solution)/shard_map/all_to_all | solution.py:52
  50.7 0.5 fusion.47
  51.2 0.3 fusion.24
  51.5 0.6 fusion.13
  52.1 0.9 %copy.31 = bf16[1,1,128,512]{3,1,2,0:T(2,128)(2,1)} copy(bf16[1,1,128,512]{3,2,1,0:T(8,128)(2,1)S(1)} %fusion.13) | data formatting | bytes 262144
  53.0 17.6 %all-to-all-done.1 = bf16[16,4,7168]{2,1,0:T(4,128)(2,1)S(1)} async-done(((bf16[16,4,7168]{2,1,0:T(4,128)(2,1)}), bf16[16,4,7168]{2,1,0:T(4,128)(2,1)S(1)}, u32[]{:S(2)}, u32[]{:S(2)}) %all-to-all-start.1) | async-done | bytes 917536 | tf_op jit(solution)/shard_map/all_to_all | solution.py:52
  70.6 0.5 copy.27
  71.1 0.9 %gather_fusion.1 = bf16[8,4,7168]{2,1,0:T(4,128)(2,1)S(1)} fusion(bf16[4,4,4,7168]{3,1,2,0:T(4,128)(2,1)S(1)} %copy.27, s32[8]{0:T(128)S(1)} %fusion.45), kind=kCustom, calls=%fused_computation.1 | custom fusion | bytes 917568 | tf_op jit(solution)/shard_map/gather | solution.py:54
  72.0 0.6 reduce_sum.75
  72.6 0.2 reshape.184
  72.8 1.0 %multiply_reduce_fusion = bf16[4,7168]{1,0:T(4,128)(2,1)} fusion(f32[4,2,7168]{2,1,0:T(2,128)S(1)} %reshape.184, f32[4,2]{1,0:T(4,128)S(1)} %copy.28), kind=kLoop, calls=%fused_computation.23 | loop fusion | flops 86016 | bytes 286752 | tf_op jit(solution)/shard_map/reduce_sum | solution.py:58
  (23 shorter events, 0.7 us)
Async XLA Ops:
  0.6 50.0 %copy-start = (bf16[1,128,576]{1,2,0:T(8,128)(2,1)S(1)}, bf16[1,128,576]{1,2,0:T(8,128)(2,1)}, u32[]{:S(2)}) copy-start(bf16[1,128,576]{1,2,0:T(8,128)(2,1)} %param.17) | copy-start | bytes 442372
  44.0 5.9 %copy-start.2 = (f32[4,2]{0,1:T(2,128)S(1)}, f32[4,2]{0,1:T(2,128)}, u32[]{:S(2)}) copy-start(f32[4,2]{0,1:T(2,128)} %param.12) | copy-start | bytes 100
  44.0 6.6 %copy-start.1 = (bf16[1,1280,576]{1,2,0:T(8,128)(2,1)S(1)}, bf16[1,1280,576]{1,2,0:T(8,128)(2,1)}, u32[]{:S(2)}) copy-start(bf16[1,1280,576]{1,2,0:T(8,128)(2,1)} %param.18) | copy-start | bytes 4423684
  45.3 25.3 %all-to-all-start.1 = ((bf16[16,4,7168]{2,1,0:T(4,128)(2,1)}), bf16[16,4,7168]{2,1,0:T(4,128)(2,1)S(1)}, u32[]{:S(2)}, u32[]{:S(2)}) async-start(bf16[16,4,7168]{2,1,0:T(4,128)(2,1)} %reshape.174), calls=%async_computation.1 | async-start | bytes 1835008 | tf_op jit(solution)/shard_map/all_to_all | solution.py:52
where the time goes:
time: 74.8 us; the launch traced here: 73.8 us
  blocking collectives  29.7 us (40%)
  waiting for transfers between devices  17.6 us (24%)
  matrix products  9.32 us (12%)
  local copies, waits for them, and re-layouts  6.13 us (8%)
  other arithmetic  5.08 us (7%)
  starting transfers between devices  4.48 us (6%)
  between operations  1.43 us (2%)
    all_to_all x1, blocking collectives, per_device(): lax.all_to_all(outgoing, 'node', split_axis=0, concat_axis=0, tiled=True)  29.7 us
    all_to_all x1, waiting for transfers between devices, per_device(): lax.all_to_all(send_result, 'node', split_axis=0, concat_axis=0, tiled=True)  17.6 us
    dot_general x1, matrix products, per_device(): jnp.dot(hidden, w_down[0], preferred_element_type=jnp.float32)  5.45 us
    all_to_all x1, starting transfers between devices, per_device(): lax.all_to_all(send_result, 'node', split_axis=0, concat_axis=0, tiled=True)  4.48 us
    dot_general x1, matrix products, per_device(): jnp.dot(flat_rows, w_gate[0], preferred_element_type=jnp.float32)  2.75 us
    unnamed x8, local copies, waits for them, and re-layouts  1.73 us
  transfers between devices with their start and end apart: 1, of which 1 were waited for; matrix products, arithmetic and copies ran while one was open for 3% of the time, Pallas kernels for 0%

commit v1 on v0

v1 whole, which is shorter than its diff:
```python
import functools

import jax
import jax.numpy as jnp
from jax import lax
from jax.experimental import pallas as pl
from jax.experimental.pallas import tpu as pltpu
from jax.sharding import PartitionSpec as P

SPLIT = 4
VALUE_DIM = 512
CHUNKS = 4
BACK_CHUNKS = 4

norm_eps = 1e-06
route_scale = 2.5
softmax_scale = 192.0 ** (-0.5)
MESH = pl.DeviceIdType.MESH
f32 = jnp.float32
bf16 = jnp.bfloat16


def kernel(
    slots,
    tok_ref, gain_ref, routes_ref, gates_ref, len_ref,
    wg_hbm, wu_hbm, wd_hbm, q_hbm, cache_hbm,
    moe_ref, att_hbm,
    wg, wu, wd, qv, cv, av, probs,
    rows, asm32, full, gate_acc, up_acc,
    part, from_core, own32, to_x, from_x, split32, outgoing, back,
    w_sem, l_sem,
    s1_send, s1_recv, c_send, c_recv, x_send, x_recv, f_send, f_recv,
    ra_send, ra_recv, rb_send, rb_recv, rc_send, rc_recv,
):
    node = lax.axis_index("node")
    slot = lax.div(node, SPLIT)
    piece = lax.rem(node, SPLIT)
    core = lax.rem(piece, 2)
    chip = lax.div(piece, 2)
    piece_c = piece + 1 - 2 * core
    piece_x = piece + 2 - 4 * chip
    piece_d = piece_c + 2 - 4 * chip
    node_c = slot * SPLIT + piece_c
    node_x = slot * SPLIT + piece_x
    row_count, width = tok_ref.shape
    cols = width // CHUNKS
    back_cols = width // BACK_CHUNKS
    block = row_count * slots
    others = [lax.rem(slot + step, slots) for step in range(1, slots)]

    def remote(src, dst, send, recv, target):
        return pltpu.make_async_remote_copy(
            src_ref=src, dst_ref=dst, send_sem=send, recv_sem=recv,
            device_id={"node": target}, device_id_type=MESH,
        )

    load_q = pltpu.make_async_copy(q_hbm.at[0], qv, l_sem.at[0])
    load_c = pltpu.make_async_copy(cache_hbm.at[0], cv, l_sem.at[1])
    load_wd = pltpu.make_async_copy(wd_hbm.at[0], wd, l_sem.at[2])
    store_a = pltpu.make_async_copy(av, att_hbm.at[0], l_sem.at[3])
    barrier = pltpu.get_barrier_semaphore()
    for other in others:
        pl.semaphore_signal(barrier, inc=1, device_id={"node": other * SPLIT + piece}, device_id_type=MESH)
    for target in (node_c, node_x):
        pl.semaphore_signal(barrier, inc=1, device_id={"node": target}, device_id_type=MESH)
    load_q.start()
    load_c.start()
    w_loads = []
    for k in range(CHUNKS):
        span = pl.ds(k * cols, cols)
        pair = (
            pltpu.make_async_copy(wg_hbm.at[0, span], wg.at[span], w_sem.at[0, k]),
            pltpu.make_async_copy(wu_hbm.at[0, span], wu.at[span], w_sem.at[1, k]),
        )
        for copy in pair:
            copy.start()
        w_loads.append(pair)
    load_wd.start()

    hidden_in = tok_ref[...].astype(f32)
    inverse = lax.rsqrt(jnp.mean(hidden_in * hidden_in, axis=-1, keepdims=True) + norm_eps)
    normed = (hidden_in * inverse * gain_ref[...].astype(f32)).astype(bf16)
    for k in range(CHUNKS):
        rows[k, slot] = normed[:, k * cols:(k + 1) * cols]
    pl.semaphore_wait(barrier, slots + 1)

    def s1(k, source, target):
        return remote(
            rows.at[k, source], rows.at[k, source],
            s1_send.at[k, target], s1_recv.at[k, source], target * SPLIT + piece,
        )

    for k in range(CHUNKS):
        for other in others:
            s1(k, slot, other).start()

    load_q.wait()
    load_c.wait()
    scores = lax.dot_general(
        qv[...], cv[...], (((1,), (1,)), ((), ())), preferred_element_type=f32
    ) * softmax_scale
    valid = lax.broadcasted_iota(jnp.int32, scores.shape, 1) < len_ref[0]
    scores = jnp.where(valid, scores, -jnp.inf)
    weights = jnp.exp(scores - jnp.max(scores, axis=-1, keepdims=True))
    total = jnp.sum(weights, axis=-1, keepdims=True)
    probs[...] = (weights / total).astype(bf16)

    def to_core(k):
        return remote(full.at[k, piece], full.at[k, piece], c_send.at[k], c_recv.at[k], node_c)

    def to_chip(k):
        return remote(full.at[k, piece], full.at[k, piece], x_send.at[k], x_recv.at[k], node_x)

    def forward(k):
        return remote(full.at[k, piece_x], full.at[k, piece_x], f_send.at[k], f_recv.at[k], node_c)

    def gather(k):
        for other in others:
            s1(k, other, other).wait_recv()
        for s in range(slots):
            asm32[k % 2, pl.ds(s * row_count, row_count), :] = rows[k, s].astype(f32)
        full[k, piece] = asm32[k % 2].astype(bf16)
        to_chip(k).start()
        to_core(k).start()

    def pass_on(k):
        to_chip(k).wait_recv()
        forward(k).start()

    def project(k):
        to_core(k).wait_recv()
        forward(k).wait_recv()
        for copy in w_loads[k]:
            copy.wait()
        x = full[k].reshape(SPLIT * block, cols)
        gate_part = jnp.dot(x, wg[pl.ds(k * cols, cols), :], preferred_element_type=f32)
        up_part = jnp.dot(x, wu[pl.ds(k * cols, cols), :], preferred_element_type=f32)
        if k == 0:
            gate_acc[...] = gate_part
            up_acc[...] = up_part
        else:
            gate_acc[...] += gate_part
            up_acc[...] += up_part

    for k in range(CHUNKS):
        gather(k)
        if k >= 1:
            pass_on(k - 1)
    av[...] = jnp.dot(probs[...], cv[:, :VALUE_DIM], preferred_element_type=f32).astype(bf16)
    store_a.start()
    pass_on(CHUNKS - 1)
    for k in range(CHUNKS):
        project(k)
    gate = gate_acc[...]
    hidden = (gate / (1.0 + jnp.exp(-gate)) * up_acc[...]).astype(bf16)
    load_wd.wait()

    def ra(j):
        return remote(part.at[j, 1 - core], from_core.at[j], ra_send.at[j], ra_recv.at[j], node_c)

    def rb(j):
        return remote(to_x.at[j], from_x.at[j], rb_send.at[j], rb_recv.at[j], node_x)

    def rc(j, origin, target):
        return remote(
            outgoing.at[j, target], back.at[j, origin],
            rc_send.at[j, target], rc_recv.at[j, origin], target * SPLIT + piece,
        )

    def down(j):
        result = jnp.dot(
            hidden, wd[:, pl.ds(j * back_cols, back_cols)], preferred_element_type=f32
        ).astype(bf16)
        for p in range(SPLIT):
            part[j, p % 2, p // 2] = result[p * block:(p + 1) * block]
        ra(j).start()

    def sum_core(j):
        ra(j).wait_recv()
        to_x[j] = (
            part[j, core, 1 - chip].astype(f32) + from_core[j, 1 - chip].astype(f32)
        ).astype(bf16)
        rb(j).start()
        own32[j] = part[j, core, chip].astype(f32) + from_core[j, chip].astype(f32)

    def sum_chip(j):
        rb(j).wait_recv()
        split32[j % 2] = own32[j] + from_x[j].astype(f32)
        for s in range(slots):
            outgoing[j, s] = split32[j % 2, pl.ds(s * row_count, row_count), :].astype(bf16)
        for other in others:
            rc(j, slot, other).start()

    picks = routes_ref[...]
    mixing = gates_ref[...]
    mixing = route_scale * mixing / jnp.sum(mixing, axis=-1, keepdims=True)

    def share(s):
        return jnp.sum(jnp.where(picks == s, mixing, 0.0), axis=-1, keepdims=True)

    def finish(j):
        for other in others:
            rc(j, other, other).wait_recv()
        back[j, slot] = outgoing[j, slot]
        moe = share(0) * back[j, 0].astype(f32)
        for s in range(1, slots):
            moe += share(s) * back[j, s].astype(f32)
        moe_ref[:, pl.ds(j * back_cols, back_cols)] = moe.astype(bf16)

    for j in range(BACK_CHUNKS):
        down(j)
        if j >= 1:
            sum_core(j - 1)
    sum_core(BACK_CHUNKS - 1)
    for j in range(BACK_CHUNKS):
        sum_chip(j)
    for j in range(BACK_CHUNKS):
        finish(j)

    for k in range(CHUNKS):
        for other in others:
            s1(k, slot, other).wait_send()
        to_core(k).wait_send()
        to_chip(k).wait_send()
        forward(k).wait_send()
    for j in range(BACK_CHUNKS):
        ra(j).wait_send()
        rb(j).wait_send()
        for other in others:
            rc(j, slot, other).wait_send()
    store_a.wait()


def per_device(tokens, routes, gates, norm_gain, w_gate, w_up, w_down, queries, cache, lengths):
    slots = lax.axis_size("node") // SPLIT
    row_count, width = tokens.shape
    units = w_gate.shape[2]
    _, heads, latent = queries.shape
    cache_len = cache.shape[1]
    block = row_count * slots
    cols = width // CHUNKS
    back_cols = width // BACK_CHUNKS
    vmem = pl.BlockSpec(memory_space=pltpu.VMEM)
    hbm = pl.BlockSpec(memory_space=pltpu.HBM)
    dma = pltpu.SemaphoreType.DMA
    moe_out, attended = pl.pallas_call(
        functools.partial(kernel, slots),
        out_shape=(
            jax.ShapeDtypeStruct((row_count, width), bf16),
            jax.ShapeDtypeStruct((1, heads, VALUE_DIM), bf16),
        ),
        in_specs=[vmem] * 4 + [pl.BlockSpec(memory_space=pltpu.SMEM)] + [hbm] * 5,
        out_specs=(vmem, hbm),
        scratch_shapes=[
            pltpu.VMEM((width, units), bf16),
            pltpu.VMEM((width, units), bf16),
            pltpu.VMEM((units, width), bf16),
            pltpu.VMEM((heads, latent), bf16),
            pltpu.VMEM((cache_len, latent), bf16),
            pltpu.VMEM((heads, VALUE_DIM), bf16),
            pltpu.VMEM((heads, cache_len), bf16),
            pltpu.VMEM((CHUNKS, slots, row_count, cols), bf16),
            pltpu.VMEM((2, block, cols), f32),
            pltpu.VMEM((CHUNKS, SPLIT, block, cols), bf16),
            pltpu.VMEM((SPLIT * block, units), f32),
            pltpu.VMEM((SPLIT * block, units), f32),
            pltpu.VMEM((BACK_CHUNKS, 2, 2, block, back_cols), bf16),
            pltpu.VMEM((BACK_CHUNKS, 2, block, back_cols), bf16),
            pltpu.VMEM((BACK_CHUNKS, block, back_cols), f32),
            pltpu.VMEM((BACK_CHUNKS, block, back_cols), bf16),
            pltpu.VMEM((BACK_CHUNKS, block, back_cols), bf16),
            pltpu.VMEM((2, block, back_cols), f32),
            pltpu.VMEM((BACK_CHUNKS, slots, row_count, back_cols), bf16),
            pltpu.VMEM((BACK_CHUNKS, slots, row_count, back_cols), bf16),
            dma((2, CHUNKS)),
            dma((4,)),
            dma((CHUNKS, slots)),
            dma((CHUNKS, slots)),
            dma((CHUNKS,)), dma((CHUNKS,)),
            dma((CHUNKS,)), dma((CHUNKS,)),
            dma((CHUNKS,)), dma((CHUNKS,)),
            dma((BACK_CHUNKS,)), dma((BACK_CHUNKS,)),
            dma((BACK_CHUNKS,)), dma((BACK_CHUNKS,)),
            dma((BACK_CHUNKS, slots)), dma((BACK_CHUNKS, slots)),
        ],
        compiler_params=pltpu.CompilerParams(
            collective_id=0, has_side_effects=True, vmem_limit_bytes=58 * 1024 * 1024
        ),
    )(
        tokens, norm_gain.reshape(1, width), routes, gates, lengths,
        w_gate, w_up, w_down, queries, cache,
    )
    return (moe_out, attended.reshape(1, heads * VALUE_DIM))


def solution(mesh):
    in_specs = (
        P(("grp", "node"), None),
        P(("grp", "node"), None),
        P(("grp", "node"), None),
        P(),
        P("node", None, None),
        P("node", None, None),
        P("node", None, None),
        P(("grp", "node"), None, None),
        P(("grp", "node"), None, None),
        P(("grp", "node")),
    )
    out_specs = (P(("grp", "node"), None), P(("grp", "node"), None))
    return jax.shard_map(
        per_device, mesh=mesh, in_specs=in_specs, out_specs=out_specs, check_vma=False
    )
```

time: 74.8 us -> 47.4 us (0.63)
  Pallas kernels: 0 us -> 34.1 us
  blocking collectives: 29.7 us -> 0 us
  waiting for transfers between devices: 17.6 us -> 0 us
  matrix products: 9.32 us -> 0 us
  local copies, waits for them, and re-layouts: 6.13 us -> 11.7 us
  other arithmetic: 5.08 us -> 0 us
  starting transfers between devices: 4.48 us -> 0 us
    pallas_call x0 -> x1, Pallas kernels: none -> 34.1 us  [per_device(): pl.pallas_call(functools.partial(kernel, slots), out_shape=(jax.ShapeDtyp...]
    all_to_all x1 -> x0, blocking collectives: 29.7 us -> none  [per_device(): lax.all_to_all(outgoing, 'node', split_axis=0, concat_axis=0, tiled=True)]
    all_to_all x1 -> x0, waiting for transfers between devices: 17.6 us -> none  [per_device(): lax.all_to_all(send_result, 'node', split_axis=0, concat_axis=0, tiled=True)]
    dot_general x4 -> x0, matrix products: 9.32 us -> none  [the longest x1 5.45 us: per_device(): jnp.dot(hidden, w_down[0], preferred_element_type=jnp.float32)]
    unnamed x8 -> x6, local copies, waits for them, and re-layouts: 1.73 us -> 10.3 us
    all_to_all x1 -> x0, starting transfers between devices: 4.48 us -> none  [per_device(): lax.all_to_all(send_result, 'node', split_axis=0, concat_axis=0, tiled=True)]
    reduce_sum x7 -> x0, other arithmetic: 2.94 us -> none  [the longest x1 0.99 us: per_device(): jnp.mean(hidden_in * hidden_in, axis=-1, keepdims=True) + norm_eps]
    gather x3 -> x0, local copies, waits for them, and re-layouts: 1.72 us -> none  [the longest x1 0.94 us: per_device(): pieces = grouped[picks_flat, :, rank_in]]
  transfers between devices with their start and end apart: 1 -> 0, of which waited for: 1 -> 0; matrix products, arithmetic and copies ran while one was open for 3% -> 0% of each run, Pallas kernels for 0% -> 0%
where the time goes in v1:
time: 47.4 us; the launch traced here: 47 us
  Pallas kernels  34.1 us (72%)
  local copies, waits for them, and re-layouts  11.7 us (25%)
  between operations  1.29 us (3%)
    pallas_call x1, Pallas kernels, per_device(): pl.pallas_call(functools.partial(kernel, slots), out_shape=(jax.ShapeDtyp...  34.1 us
    unnamed x6, local copies, waits for them, and re-layouts  10.3 us
    reshape x1, local copies, waits for them, and re-layouts, per_device(): norm_gain.reshape(1, width)  1.34 us

profile of v1, /device:TPU:0, one launch (start us, length us, event | category | flops | bytes accessed | tf_op | source)
XLA Modules:
  0.0 47.0 jit_solution(7034560750718813018)
XLA Ops:
  1.3 1.3 %copy.12.routes_ref = s32[4,2]{1,0:T(4,128)} copy(s32[4,2]{0,1:T(2,128)} %param.11) | data formatting | bytes 64 | tf_op args[1]
  2.6 1.3 %copy.13.gates_ref = f32[4,2]{1,0:T(4,128)} copy(f32[4,2]{0,1:T(2,128)} %param.12) | data formatting | bytes 64 | tf_op args[2]
  4.0 1.3 %reshape.10.gain_ref = bf16[1,7168]{1,0:T(2,128)(2,1)} reshape(bf16[7168]{0:T(1024)(128)(2,1)} %param.13) | data formatting | bytes 28672 | tf_op jit(solution)/shard_map/reshape | solution.py:290
  5.3 1.7 %copy.14.q_hbm = bf16[1,128,576]{2,1,0:T(8,128)(2,1)} copy(bf16[1,128,576]{1,2,0:T(8,128)(2,1)} %param.17) | data formatting | bytes 294912 | tf_op args[7]
  7.0 2.7 %copy.15.cache_hbm = bf16[1,1280,576]{2,1,0:T(8,128)(2,1)} copy(bf16[1,1280,576]{1,2,0:T(8,128)(2,1)} %param.18) | data formatting | bytes 2949120 | tf_op args[8]
  9.7 34.1 %shard_map.113 = (bf16[4,7168]{1,0:T(4,128)(2,1)}, bf16[1,128,512]{2,1,0:T(8,128)(2,1)}) custom-call(bf16[4,7168]{1,0:T(4,128)(2,1)} %tok_ref.1, bf16[1,7168]{1,0:T(2,128)(2,1)} %reshape.10.gain_ref, s32[4,2]{1,0:T(4,128)} %copy.12.routes_ref, f32[4,2]{1,0:T(4,128)} %copy.13.gates_ref, s32[1]{0:T(128)S(6)} %copy.18.len_ref, bf16[1,7168,256]{2,1,0:T(8,128)(2,1)} %wg_hbm.1, ...), custom_call_target="tpu_custom_call" | custom-call | tf_op jit(solution)/shard_map/pallas_call | solution.py:246
  43.8 1.8 %copy.16 = bf16[1,1,128,512]{3,1,2,0:T(2,128)(2,1)} copy(bf16[1,1,128,512]{3,2,1,0:T(8,128)(2,1)} %bitcast.3) | data formatting | bytes 262144
  45.6 1.5 %copy.19 = bf16[4,7168]{1,0:T(4,128)(2,1)} copy(bf16[4,7168]{1,0:T(4,128)(2,1)} %get-tuple-element.8) | data formatting | bytes 114688

commit v2 on v1

--- a/solution.py
+++ b/solution.py
@@ -11,6 +11,7 @@
 VALUE_DIM = 512
 CHUNKS = 4
 BACK_CHUNKS = 4
+LANES = 128
 
 norm_eps = 1e-06
 route_scale = 2.5
@@ -79,9 +80,14 @@
 
     hidden_in = tok_ref[...].astype(f32)
     inverse = lax.rsqrt(jnp.mean(hidden_in * hidden_in, axis=-1, keepdims=True) + norm_eps)
-    normed = (hidden_in * inverse * gain_ref[...].astype(f32)).astype(bf16)
-    for k in range(CHUNKS):
-        rows[k, slot] = normed[:, k * cols:(k + 1) * cols]
+    gain = gain_ref[...].astype(f32)
+    for k in range(CHUNKS):
+        for lane in range(0, cols, LANES):
+            start = k * cols + lane
+            here = start // LANES
+            rows[k, slot, :, lane:lane + LANES] = (
+                hidden_in[:, start:start + LANES] * inverse * gain[here:here + 1]
+            ).astype(bf16)
     pl.semaphore_wait(barrier, slots + 1)
 
     def s1(k, source, target):
@@ -97,7 +103,7 @@
     load_q.wait()
     load_c.wait()
     scores = lax.dot_general(
-        qv[...], cv[...], (((1,), (1,)), ((), ())), preferred_element_type=f32
+        qv[...], cv[...], (((0,), (0,)), ((), ())), preferred_element_type=f32
     ) * softmax_scale
     valid = lax.broadcasted_iota(jnp.int32, scores.shape, 1) < len_ref[0]
     scores = jnp.where(valid, scores, -jnp.inf)
@@ -146,7 +152,9 @@
         gather(k)
         if k >= 1:
             pass_on(k - 1)
-    av[...] = jnp.dot(probs[...], cv[:, :VALUE_DIM], preferred_element_type=f32).astype(bf16)
+    av[...] = lax.dot_general(
+        probs[...], cv[:VALUE_DIM, :], (((1,), (1,)), ((), ())), preferred_element_type=f32
+    ).astype(bf16)
     store_a.start()
     pass_on(CHUNKS - 1)
     for k in range(CHUNKS):
@@ -193,18 +201,26 @@
 
     picks = routes_ref[...]
     mixing = gates_ref[...]
-    mixing = route_scale * mixing / jnp.sum(mixing, axis=-1, keepdims=True)
+    mixing = route_scale * mixing / jnp.sum(mixing, axis=0, keepdims=True)
+    diagonal = (
+        lax.broadcasted_iota(jnp.int32, (row_count, row_count), 0)
+        == lax.broadcasted_iota(jnp.int32, (row_count, row_count), 1)
+    )
 
     def share(s):
-        return jnp.sum(jnp.where(picks == s, mixing, 0.0), axis=-1, keepdims=True)
+        line = jnp.sum(jnp.where(picks == s, mixing, 0.0), axis=0, keepdims=True)
+        line = jnp.broadcast_to(line, (row_count, row_count))
+        return jnp.sum(jnp.where(diagonal, line, 0.0), axis=1, keepdims=True)
+
+    shares = [share(s) for s in range(slots)]
 
     def finish(j):
         for other in others:
             rc(j, other, other).wait_recv()
         back[j, slot] = outgoing[j, slot]
-        moe = share(0) * back[j, 0].astype(f32)
+        moe = shares[0] * back[j, 0].astype(f32)
         for s in range(1, slots):
-            moe += share(s) * back[j, s].astype(f32)
+            moe += shares[s] * back[j, s].astype(f32)
         moe_ref[:, pl.ds(j * back_cols, back_cols)] = moe.astype(bf16)
 
     for j in range(BACK_CHUNKS):
@@ -255,8 +271,8 @@
             pltpu.VMEM((width, units), bf16),
             pltpu.VMEM((width, units), bf16),
             pltpu.VMEM((units, width), bf16),
-            pltpu.VMEM((heads, latent), bf16),
-            pltpu.VMEM((cache_len, latent), bf16),
+            pltpu.VMEM((latent, heads), bf16),
+            pltpu.VMEM((latent, cache_len), bf16),
             pltpu.VMEM((heads, VALUE_DIM), bf16),
             pltpu.VMEM((heads, cache_len), bf16),
             pltpu.VMEM((CHUNKS, slots, row_count, cols), bf16),
@@ -287,8 +303,8 @@
             collective_id=0, has_side_effects=True, vmem_limit_bytes=58 * 1024 * 1024
         ),
     )(
-        tokens, norm_gain.reshape(1, width), routes, gates, lengths,
-        w_gate, w_up, w_down, queries, cache,
+        tokens, norm_gain.reshape(width // LANES, LANES), routes.T, gates.T, lengths,
+        w_gate, w_up, w_down, queries.swapaxes(1, 2), cache.swapaxes(1, 2),
     )
     return (moe_out, attended.reshape(1, heads * VALUE_DIM))
 

time: 47.4 us -> 38.9 us (0.82)
  local copies, waits for them, and re-layouts: 11.7 us -> 3.27 us
    unnamed x6 -> x2, local copies, waits for them, and re-layouts: 10.3 us -> 3.27 us
    reshape x1 -> x0, local copies, waits for them, and re-layouts: 1.34 us -> none  [per_device(): norm_gain.reshape(1, width)]
where the time goes in v2:
time: 38.9 us; the launch traced here: 38.6 us
  Pallas kernels  34.1 us (88%)
  local copies, waits for them, and re-layouts  3.27 us (8%)
  between operations  1.29 us (3%)
    pallas_call x1, Pallas kernels, per_device(): pl.pallas_call(functools.partial(kernel, slots), out_shape=(jax.ShapeDtyp...  34.1 us
    unnamed x2, local copies, waits for them, and re-layouts  3.27 us

profile of v2, /device:TPU:0, one launch (start us, length us, event | category | flops | bytes accessed | tf_op | source)
XLA Modules:
  0.0 38.6 jit_solution(5382022339044961498)
XLA Ops:
  1.3 34.1 %shard_map.113 = (bf16[4,7168]{1,0:T(4,128)(2,1)}, bf16[1,128,512]{2,1,0:T(8,128)(2,1)}) custom-call(bf16[4,7168]{1,0:T(4,128)(2,1)} %tok_ref.1, bf16[56,128]{1,0:T(8,128)(2,1)} %bitcast.11, s32[2,4]{1,0:T(2,128)} %bitcast.12, f32[2,4]{1,0:T(2,128)} %bitcast.13, s32[1]{0:T(128)S(6)} %copy.14.len_ref, bf16[1,7168,256]{2,1,0:T(8,128)(2,1)} %wg_hbm.1, ...), custom_call_target="tpu_custom_call" | custom-call | tf_op jit(solution)/shard_map/pallas_call | solution.py:262
  35.4 1.8 %copy.12 = bf16[1,1,128,512]{3,1,2,0:T(2,128)(2,1)} copy(bf16[1,1,128,512]{3,2,1,0:T(8,128)(2,1)} %bitcast.10) | data formatting | bytes 262144
  37.2 1.5 %copy.15 = bf16[4,7168]{1,0:T(4,128)(2,1)} copy(bf16[4,7168]{1,0:T(4,128)(2,1)} %get-tuple-element.8) | data formatting | bytes 114688

commit v3 on v2

--- a/solution.py
+++ b/solution.py
@@ -10,7 +10,8 @@
 SPLIT = 4
 VALUE_DIM = 512
 CHUNKS = 4
-BACK_CHUNKS = 4
+BACK_CHUNKS = 2
+WINDOW = 3
 LANES = 128
 
 norm_eps = 1e-06
@@ -21,13 +22,25 @@
 bf16 = jnp.bfloat16
 
 
+def slot_order(slot, slots):
+    if slots & (slots - 1):
+        return [lax.rem(slot + step, slots) for step in range(slots)]
+    order = [slot]
+    bit = 1
+    while bit < slots:
+        flip = [s + bit - 2 * bit * lax.rem(lax.div(s, bit), 2) for s in order]
+        order = order + flip
+        bit *= 2
+    return order
+
+
 def kernel(
     slots,
     tok_ref, gain_ref, routes_ref, gates_ref, len_ref,
     wg_hbm, wu_hbm, wd_hbm, q_hbm, cache_hbm,
     moe_ref, att_hbm,
     wg, wu, wd, qv, cv, av, probs,
-    rows, asm32, full, gate_acc, up_acc,
+    rows, asm32, gate_acc, up_acc,
     part, from_core, own32, to_x, from_x, split32, outgoing, back,
     w_sem, l_sem,
     s1_send, s1_recv, c_send, c_recv, x_send, x_recv, f_send, f_recv,
@@ -47,7 +60,8 @@
     cols = width // CHUNKS
     back_cols = width // BACK_CHUNKS
     block = row_count * slots
-    others = [lax.rem(slot + step, slots) for step in range(1, slots)]
+    order = slot_order(slot, slots)
+    others = order[1:]
 
     def remote(src, dst, send, recv, target):
         return pltpu.make_async_remote_copy(
@@ -85,20 +99,30 @@
         for lane in range(0, cols, LANES):
             start = k * cols + lane
             here = start // LANES
-            rows[k, slot, :, lane:lane + LANES] = (
+            rows[piece, slot, :, start:start + LANES] = (
                 hidden_in[:, start:start + LANES] * inverse * gain[here:here + 1]
             ).astype(bf16)
     pl.semaphore_wait(barrier, slots + 1)
 
-    def s1(k, source, target):
+    def s1(source, target):
         return remote(
-            rows.at[k, source], rows.at[k, source],
-            s1_send.at[k, target], s1_recv.at[k, source], target * SPLIT + piece,
+            rows.at[piece, source], rows.at[piece, source],
+            s1_send.at[target], s1_recv.at[source], target * SPLIT + piece,
         )
 
-    for k in range(CHUNKS):
-        for other in others:
-            s1(k, slot, other).start()
+    def to_core(s):
+        return remote(rows.at[piece, s], rows.at[piece, s], c_send.at[s], c_recv.at[s], node_c)
+
+    def to_chip(s):
+        return remote(rows.at[piece, s], rows.at[piece, s], x_send.at[s], x_recv.at[s], node_x)
+
+    def forward(s):
+        return remote(rows.at[piece_x, s], rows.at[piece_x, s], f_send.at[s], f_recv.at[s], node_c)
+
+    for other in others:
+        s1(slot, other).start()
+    to_chip(slot).start()
+    to_core(slot).start()
 
     load_q.wait()
     load_c.wait()
@@ -111,34 +135,30 @@
     total = jnp.sum(weights, axis=-1, keepdims=True)
     probs[...] = (weights / total).astype(bf16)
 
-    def to_core(k):
-        return remote(full.at[k, piece], full.at[k, piece], c_send.at[k], c_recv.at[k], node_c)
-
-    def to_chip(k):
-        return remote(full.at[k, piece], full.at[k, piece], x_send.at[k], x_recv.at[k], node_x)
-
-    def forward(k):
-        return remote(full.at[k, piece_x], full.at[k, piece_x], f_send.at[k], f_recv.at[k], node_c)
-
-    def gather(k):
-        for other in others:
-            s1(k, other, other).wait_recv()
-        for s in range(slots):
-            asm32[k % 2, pl.ds(s * row_count, row_count), :] = rows[k, s].astype(f32)
-        full[k, piece] = asm32[k % 2].astype(bf16)
-        to_chip(k).start()
-        to_core(k).start()
-
-    def pass_on(k):
-        to_chip(k).wait_recv()
-        forward(k).start()
-
-    def project(k):
-        to_core(k).wait_recv()
-        forward(k).wait_recv()
+    for i in range(1, slots):
+        s1(order[i], order[i]).wait_recv()
+        to_chip(order[i]).start()
+        to_core(order[i]).start()
+        to_chip(order[i - 1]).wait_recv()
+        forward(order[i - 1]).start()
+    av[...] = lax.dot_general(
+        probs[...], cv[:VALUE_DIM, :], (((1,), (1,)), ((), ())), preferred_element_type=f32
+    ).astype(bf16)
+    store_a.start()
+    to_chip(order[-1]).wait_recv()
+    forward(order[-1]).start()
+    for s in order:
+        to_core(s).wait_recv()
+        forward(s).wait_recv()
+    for k in range(CHUNKS):
+        for p in range(SPLIT):
+            for s in range(slots):
+                asm32[k % 2, pl.ds((p * slots + s) * row_count, row_count), :] = (
+                    rows[p, s, :, pl.ds(k * cols, cols)].astype(f32)
+                )
+        x = asm32[k % 2].astype(bf16)
         for copy in w_loads[k]:
             copy.wait()
-        x = full[k].reshape(SPLIT * block, cols)
         gate_part = jnp.dot(x, wg[pl.ds(k * cols, cols), :], preferred_element_type=f32)
         up_part = jnp.dot(x, wu[pl.ds(k * cols, cols), :], preferred_element_type=f32)
         if k == 0:
@@ -147,18 +167,6 @@
         else:
             gate_acc[...] += gate_part
             up_acc[...] += up_part
-
-    for k in range(CHUNKS):
-        gather(k)
-        if k >= 1:
-            pass_on(k - 1)
-    av[...] = lax.dot_general(
-        probs[...], cv[:VALUE_DIM, :], (((1,), (1,)), ((), ())), preferred_element_type=f32
-    ).astype(bf16)
-    store_a.start()
-    pass_on(CHUNKS - 1)
-    for k in range(CHUNKS):
-        project(k)
     gate = gate_acc[...]
     hidden = (gate / (1.0 + jnp.exp(-gate)) * up_acc[...]).astype(bf16)
     load_wd.wait()
@@ -166,13 +174,13 @@
     def ra(j):
         return remote(part.at[j, 1 - core], from_core.at[j], ra_send.at[j], ra_recv.at[j], node_c)
 
-    def rb(j):
-        return remote(to_x.at[j], from_x.at[j], rb_send.at[j], rb_recv.at[j], node_x)
-
-    def rc(j, origin, target):
+    def rb(s):
+        return remote(to_x.at[s], from_x.at[s], rb_send.at[s], rb_recv.at[s], node_x)
+
+    def rc(origin, target):
         return remote(
-            outgoing.at[j, target], back.at[j, origin],
-            rc_send.at[j, target], rc_recv.at[j, origin], target * SPLIT + piece,
+            outgoing.at[target], back.at[origin],
+            rc_send.at[target], rc_recv.at[origin], target * SPLIT + piece,
         )
 
     def down(j):
@@ -185,19 +193,15 @@
 
     def sum_core(j):
         ra(j).wait_recv()
-        to_x[j] = (
-            part[j, core, 1 - chip].astype(f32) + from_core[j, 1 - chip].astype(f32)
-        ).astype(bf16)
-        rb(j).start()
-        own32[j] = part[j, core, chip].astype(f32) + from_core[j, chip].astype(f32)
-
-    def sum_chip(j):
-        rb(j).wait_recv()
-        split32[j % 2] = own32[j] + from_x[j].astype(f32)
+        span = pl.ds(j * back_cols, back_cols)
+        for side, own_side in ((0, 1 - chip), (1, chip)):
+            split32[side] = (
+                part[j, core, own_side].astype(f32) + from_core[j, own_side].astype(f32)
+            )
         for s in range(slots):
-            outgoing[j, s] = split32[j % 2, pl.ds(s * row_count, row_count), :].astype(bf16)
-        for other in others:
-            rc(j, slot, other).start()
+            here = pl.ds(s * row_count, row_count)
+            to_x[s, :, span] = split32[0, here, :].astype(bf16)
+            own32[s, :, span] = split32[1, here, :]
 
     picks = routes_ref[...]
     mixing = gates_ref[...]
@@ -214,36 +218,44 @@
 
     shares = [share(s) for s in range(slots)]
 
-    def finish(j):
-        for other in others:
-            rc(j, other, other).wait_recv()
-        back[j, slot] = outgoing[j, slot]
-        moe = shares[0] * back[j, 0].astype(f32)
+    down(0)
+    for j in range(BACK_CHUNKS):
+        if j + 1 < BACK_CHUNKS:
+            down(j + 1)
+        sum_core(j)
+    home = order[::-1]
+    for i in range(min(WINDOW, slots)):
+        rb(home[i]).start()
+    for i in range(slots):
+        s = home[i]
+        rb(s).wait_recv()
+        if i + WINDOW < slots:
+            rb(home[i + WINDOW]).start()
+        total_rows = (own32[s] + from_x[s].astype(f32)).astype(bf16)
+        if i + 1 < slots:
+            outgoing[s] = total_rows
+            rc(slot, s).start()
+        else:
+            back[slot] = total_rows
+    for other in others:
+        rc(other, other).wait_recv()
+    for j in range(BACK_CHUNKS):
+        span = pl.ds(j * back_cols, back_cols)
+        moe = shares[0] * back[0, :, span].astype(f32)
         for s in range(1, slots):
-            moe += shares[s] * back[j, s].astype(f32)
-        moe_ref[:, pl.ds(j * back_cols, back_cols)] = moe.astype(bf16)
-
-    for j in range(BACK_CHUNKS):
-        down(j)
-        if j >= 1:
-            sum_core(j - 1)
-    sum_core(BACK_CHUNKS - 1)
-    for j in range(BACK_CHUNKS):
-        sum_chip(j)
-    for j in range(BACK_CHUNKS):
-        finish(j)
-
-    for k in range(CHUNKS):
-        for other in others:
-            s1(k, slot, other).wait_send()
-        to_core(k).wait_send()
-        to_chip(k).wait_send()
-        forward(k).wait_send()
+            moe += shares[s] * back[s, :, span].astype(f32)
+        moe_ref[:, span] = moe.astype(bf16)
+
+    for other in others:
+        s1(slot, other).wait_send()
+        rc(slot, other).wait_send()
+    for s in order:
+        to_core(s).wait_send()
+        to_chip(s).wait_send()
+        forward(s).wait_send()
+        rb(s).wait_send()
     for j in range(BACK_CHUNKS):
         ra(j).wait_send()
-        rb(j).wait_send()
-        for other in others:
-            rc(j, slot, other).wait_send()
     store_a.wait()
 
 
@@ -275,29 +287,27 @@
             pltpu.VMEM((latent, cache_len), bf16),
             pltpu.VMEM((heads, VALUE_DIM), bf16),
             pltpu.VMEM((heads, cache_len), bf16),
-            pltpu.VMEM((CHUNKS, slots, row_count, cols), bf16),
-            pltpu.VMEM((2, block, cols), f32),
-            pltpu.VMEM((CHUNKS, SPLIT, block, cols), bf16),
+            pltpu.VMEM((SPLIT, slots, row_count, width), bf16),
+            pltpu.VMEM((2, SPLIT * block, cols), f32),
             pltpu.VMEM((SPLIT * block, units), f32),
             pltpu.VMEM((SPLIT * block, units), f32),
             pltpu.VMEM((BACK_CHUNKS, 2, 2, block, back_cols), bf16),
             pltpu.VMEM((BACK_CHUNKS, 2, block, back_cols), bf16),
-            pltpu.VMEM((BACK_CHUNKS, block, back_cols), f32),
-            pltpu.VMEM((BACK_CHUNKS, block, back_cols), bf16),
-            pltpu.VMEM((BACK_CHUNKS, block, back_cols), bf16),
+            pltpu.VMEM((slots, row_count, width), f32),
+            pltpu.VMEM((slots, row_count, width), bf16),
+            pltpu.VMEM((slots, row_count, width), bf16),
             pltpu.VMEM((2, block, back_cols), f32),
-            pltpu.VMEM((BACK_CHUNKS, slots, row_count, back_cols), bf16),
-            pltpu.VMEM((BACK_CHUNKS, slots, row_count, back_cols), bf16),
+            pltpu.VMEM((slots, row_count, width), bf16),
+            pltpu.VMEM((slots, row_count, width), bf16),
             dma((2, CHUNKS)),
             dma((4,)),
-            dma((CHUNKS, slots)),
-            dma((CHUNKS, slots)),
-            dma((CHUNKS,)), dma((CHUNKS,)),
-            dma((CHUNKS,)), dma((CHUNKS,)),
-            dma((CHUNKS,)), dma((CHUNKS,)),
+            dma((slots,)), dma((slots,)),
+            dma((slots,)), dma((slots,)),
+            dma((slots,)), dma((slots,)),
+            dma((slots,)), dma((slots,)),
             dma((BACK_CHUNKS,)), dma((BACK_CHUNKS,)),
-            dma((BACK_CHUNKS,)), dma((BACK_CHUNKS,)),
-            dma((BACK_CHUNKS, slots)), dma((BACK_CHUNKS, slots)),
+            dma((slots,)), dma((slots,)),
+            dma((slots,)), dma((slots,)),
         ],
         compiler_params=pltpu.CompilerParams(
             collective_id=0, has_side_effects=True, vmem_limit_bytes=58 * 1024 * 1024

time: 38.9 us -> 36.5 us (0.938)
  Pallas kernels: 34.1 us -> 31.7 us
    pallas_call x1, Pallas kernels: 34.1 us -> 31.7 us  [per_device(): pl.pallas_call(functools.partial(kernel, slots), out_shape=(jax.ShapeDtyp...]
where the time goes in v3:
time: 36.5 us; the launch traced here: 36.3 us
  Pallas kernels  31.7 us (87%)
  local copies, waits for them, and re-layouts  3.27 us (9%)
  between operations  1.29 us (4%)
    pallas_call x1, Pallas kernels, per_device(): pl.pallas_call(functools.partial(kernel, slots), out_shape=(jax.ShapeDtyp...  31.7 us
    unnamed x2, local copies, waits for them, and re-layouts  3.27 us

profile of v3, /device:TPU:0, one launch (start us, length us, event | category | flops | bytes accessed | tf_op | source)
XLA Modules:
  0.0 36.3 jit_solution(2343041558002522487)
XLA Ops:
  1.3 31.7 %shard_map.113 = (bf16[4,7168]{1,0:T(4,128)(2,1)}, bf16[1,128,512]{2,1,0:T(8,128)(2,1)}) custom-call(bf16[4,7168]{1,0:T(4,128)(2,1)} %tok_ref.1, bf16[56,128]{1,0:T(8,128)(2,1)} %bitcast.11, s32[2,4]{1,0:T(2,128)} %bitcast.12, f32[2,4]{1,0:T(2,128)} %bitcast.13, s32[1]{0:T(128)S(6)} %copy.14.len_ref, bf16[1,7168,256]{2,1,0:T(8,128)(2,1)} %wg_hbm.1, ...), custom_call_target="tpu_custom_call" | custom-call | tf_op jit(solution)/shard_map/pallas_call | solution.py:274
  33.0 1.8 %copy.12 = bf16[1,1,128,512]{3,1,2,0:T(2,128)(2,1)} copy(bf16[1,1,128,512]{3,2,1,0:T(8,128)(2,1)} %bitcast.10) | data formatting | bytes 262144
  34.8 1.5 %copy.15 = bf16[4,7168]{1,0:T(4,128)(2,1)} copy(bf16[4,7168]{1,0:T(4,128)(2,1)} %get-tuple-element.8) | data formatting | bytes 114688

commit v4 on v3

--- a/solution.py
+++ b/solution.py
@@ -191,17 +191,12 @@
             part[j, p % 2, p // 2] = result[p * block:(p + 1) * block]
         ra(j).start()
 
-    def sum_core(j):
-        ra(j).wait_recv()
+    def sum_core(j, side, own_side, kept):
         span = pl.ds(j * back_cols, back_cols)
-        for side, own_side in ((0, 1 - chip), (1, chip)):
-            split32[side] = (
-                part[j, core, own_side].astype(f32) + from_core[j, own_side].astype(f32)
-            )
+        split32[side] = part[j, core, own_side].astype(f32) + from_core[j, own_side].astype(f32)
         for s in range(slots):
             here = pl.ds(s * row_count, row_count)
-            to_x[s, :, span] = split32[0, here, :].astype(bf16)
-            own32[s, :, span] = split32[1, here, :]
+            kept[s, :, span] = split32[side, here, :].astype(kept.dtype)
 
     picks = routes_ref[...]
     mixing = gates_ref[...]
@@ -222,10 +217,13 @@
     for j in range(BACK_CHUNKS):
         if j + 1 < BACK_CHUNKS:
             down(j + 1)
-        sum_core(j)
+        ra(j).wait_recv()
+        sum_core(j, 0, 1 - chip, to_x)
     home = order[::-1]
     for i in range(min(WINDOW, slots)):
         rb(home[i]).start()
+    for j in range(BACK_CHUNKS):
+        sum_core(j, 1, chip, own32)
     for i in range(slots):
         s = home[i]
         rb(s).wait_recv()

time: 36.5 us -> 36.5 us (level)
  no operation moved by 1% of the time
where the time goes in v4:
time: 36.5 us; the launch traced here: 36.2 us
  Pallas kernels  31.7 us (87%)
  local copies, waits for them, and re-layouts  3.27 us (9%)
  between operations  1.29 us (4%)
    pallas_call x1, Pallas kernels, per_device(): pl.pallas_call(functools.partial(kernel, slots), out_shape=(jax.ShapeDtyp...  31.7 us
    unnamed x2, local copies, waits for them, and re-layouts  3.27 us

profile of v4, /device:TPU:0, one launch (start us, length us, event | category | flops | bytes accessed | tf_op | source)
XLA Modules:
  0.0 36.2 jit_solution(3508736033332947973)
XLA Ops:
  1.3 31.7 %shard_map.113 = (bf16[4,7168]{1,0:T(4,128)(2,1)}, bf16[1,128,512]{2,1,0:T(8,128)(2,1)}) custom-call(bf16[4,7168]{1,0:T(4,128)(2,1)} %tok_ref.1, bf16[56,128]{1,0:T(8,128)(2,1)} %bitcast.11, s32[2,4]{1,0:T(2,128)} %bitcast.12, f32[2,4]{1,0:T(2,128)} %bitcast.13, s32[1]{0:T(128)S(6)} %copy.14.len_ref, bf16[1,7168,256]{2,1,0:T(8,128)(2,1)} %wg_hbm.1, ...), custom_call_target="tpu_custom_call" | custom-call | tf_op jit(solution)/shard_map/pallas_call | solution.py:272
  33.0 1.8 %copy.12 = bf16[1,1,128,512]{3,1,2,0:T(2,128)(2,1)} copy(bf16[1,1,128,512]{3,2,1,0:T(8,128)(2,1)} %bitcast.10) | data formatting | bytes 262144
  34.8 1.5 %copy.15 = bf16[4,7168]{1,0:T(4,128)(2,1)} copy(bf16[4,7168]{1,0:T(4,128)(2,1)} %get-tuple-element.8) | data formatting | bytes 114688
